TPU v7x, 128 devices: a whole 4x4x4 slice. The times are simulated.
128 devices in a mesh: samp: 8 (over z, y_hi), feat: 16 (over y_lo, x, core).
Axes of the slice: x: 4, y: 4 (y_hi: 2, y_lo: 2; y = y_hi * 2 + y_lo), z: 4, core: 2. Of those that a mesh axis runs over, the one named last changes fastest.
Arguments:
- inputs: bfloat16 [440, 32768], P(None, ('samp', 'feat')), may hold values from -6 to 6
- probs: bfloat16 [147, 32768], P(None, ('samp', 'feat')), may hold values from 0 to 1, as said below
- labels: int32 [32768], P(('samp', 'feat')), may hold values from 0 to 146
- proj_weight: bfloat16 [440, 32768], P(None, ('feat', 'samp')), may hold values from -0.25 to 0.25
- phase: bfloat16 [1, 32768], P(None, ('feat', 'samp')), may hold values from -3.140625 to 3.140625
- direction: bfloat16 [147, 32768], P(None, ('feat', 'samp')), may hold values from -0.03125 to 0.03125
- damping: float32 [1], replicated, may hold values from 300 to 3000
Outputs:
- hess_vec: float32 [147, 32768], P(None, ('feat', 'samp'))
- gradient: float32 [147, 32768], P(None, ('feat', 'samp'))
Inputs may be any that keep to these rules, and one draw needn't show every extreme that they name: Each column of probs is positive and sums to one up to rounding.
All inputs are finite; a program needn't handle non-finite values.
Results may differ from a plain program's by a relative error of at most 0.005.
The roundings to bfloat16 on the way count: a program that leaves them out, or rounds other values in their place, can miss the bound.
Values may be sent and summed in bfloat16 or wider, within the bound.
A program may use at most 64 MiB of HBM per device.

v0:
```python
import jax
import jax.numpy as jnp
from jax import lax
from jax.sharding import PartitionSpec as P


def on_device(inputs, probs, labels, proj_weight, phase, direction, damping):
    classes = probs.shape[0]
    own_prob = probs.astype(jnp.float32)
    class_ids = lax.broadcasted_iota(jnp.int32, probs.shape, 0)
    onehot = (class_ids == labels[None, :]).astype(jnp.float32)
    own_resid = (own_prob - onehot).astype(jnp.bfloat16)
    w_all, phase_all, dir_all = (
        lax.all_gather(proj_weight, "samp", axis=1, tiled=True),
        lax.all_gather(phase, "samp", axis=1, tiled=True),
        lax.all_gather(direction, "samp", axis=1, tiled=True),
    )
    phase_col = phase_all.astype(jnp.float32).T
    x_all, resid_all, probs_all = (
        lax.all_gather(inputs, "feat", axis=1, tiled=True),
        lax.all_gather(own_resid, "feat", axis=1, tiled=True),
        lax.all_gather(probs, "feat", axis=1, tiled=True),
    )
    rows = x_all.shape[1]
    width = w_all.shape[1]
    block = min(512, rows)
    count = rows // block
    dims = (((1,), (1,)), ((), ()))

    def features(start):
        x_block = lax.dynamic_slice_in_dim(x_all, start, block, 1)
        proj = lax.dot_general(
            w_all, x_block, (((0,), (0,)), ((), ())), preferred_element_type=jnp.float32
        )
        return jnp.cos(proj + phase_col).astype(jnp.bfloat16)

    empty_tangent = jnp.zeros((classes, rows), jnp.float32)
    empty_block = jnp.zeros((classes, width), jnp.float32)

    def first_late(index, tangent):
        start = index * block
        feats = features(start)
        piece = jnp.dot(dir_all, feats, preferred_element_type=jnp.float32)
        return lax.dynamic_update_slice_in_dim(tangent, piece, start, 1)

    tangent = lax.fori_loop(0, count, first_late, empty_tangent)
    total = lax.psum(tangent.astype(jnp.bfloat16), "feat").astype(jnp.float32)
    prob = probs_all.astype(jnp.float32)
    mixed = jnp.sum(prob * total, axis=0, keepdims=True)
    curv_all = (prob * (total - mixed)).astype(jnp.bfloat16)

    def second_late(index, carry):
        hv_acc, grad_acc = carry
        start = index * block
        feats = features(start)
        curv_block = lax.dynamic_slice_in_dim(curv_all, start, block, 1)
        resid_block = lax.dynamic_slice_in_dim(resid_all, start, block, 1)
        hv_acc = hv_acc + lax.dot_general(
            curv_block, feats, dims, preferred_element_type=jnp.float32
        )
        grad_acc = grad_acc + lax.dot_general(
            resid_block, feats, dims, preferred_element_type=jnp.float32
        )
        return (hv_acc, grad_acc)

    hv_acc, grad_acc = lax.fori_loop(0, count, second_late, (empty_block, empty_block))
    hv_share, gradient = (
        lax.psum_scatter(hv_acc, "samp", scatter_dimension=1, tiled=True),
        lax.psum_scatter(grad_acc, "samp", scatter_dimension=1, tiled=True),
    )
    hess_vec = hv_share + damping[0] * direction.astype(jnp.float32)
    return (hess_vec, gradient)


def solution(mesh):
    placed = (
        P(None, ("samp", "feat")),
        P(None, ("samp", "feat")),
        P(("samp", "feat")),
        P(None, ("feat", "samp")),
        P(None, ("feat", "samp")),
        P(None, ("feat", "samp")),
        P(),
    )
    return jax.shard_map(
        on_device,
        mesh=mesh,
        in_specs=placed,
        out_specs=(P(None, ("feat", "samp")), P(None, ("feat", "samp"))),
        check_vma=False,
    )
```

profile of v0, /device:TPU:1, one launch (start us, length us, event | category | flops | bytes accessed | tf_op | source)
XLA Modules:
  0.0 727.9 jit_solution(17047907288443202636)
XLA Ops:
  7.2 0.0 all-gather.9.cloned.1.call-start
  7.2 0.7 all-gather.9.cloned.1.call-update
  7.9 0.0 all-gather.7.cloned.1.call-start
  7.9 0.7 all-gather.7.cloned.1.call-update
  8.6 0.0 all-gather.5.cloned.1.call-start
  8.7 0.7 all-gather.5.cloned.1.call-update
  9.4 0.0 all-reduce.2.cloned.1.call-start
  9.4 22.2 %all_gather.21 = bf16[1,2048]{1,0:T(2,128)(2,1)S(1)} all-gather(bf16[1,256]{1,0:T(2,128)(2,1)} %param.15), channel_id=1, replica_groups=mesh['samp'=8,'feat'=16] {'samp'}, dimensions={1}, use_global_device_ids=true | all-gather | bytes 4608 | tf_op jit(solution)/shard_map/all_gather | solution.py:15
  31.6 34.2 %all_gather.22 = bf16[147,2048]{1,0:T(8,128)(2,1)S(1)} all-gather(bf16[147,256]{1,0:T(8,128)(2,1)} %param.16), channel_id=1, replica_groups=mesh['samp'=8,'feat'=16] {'samp'}, dimensions={1}, use_global_device_ids=true | all-gather | bytes 677376 | tf_op jit(solution)/shard_map/all_gather | solution.py:16
  65.9 2.8 all-gather.9.cloned.1.call-done
  68.7 43.8 %all-gather.7.cloned.1.call-done = bf16[440,4096]{1,0:T(8,128)(2,1)} async-done(((bf16[440,256]{1,0:T(8,128)(2,1)}), bf16[440,4096]{1,0:T(8,128)(2,1)}) %all-gather.7.cloned.1.call-update) | async-done | bytes 3604496 | tf_op jit(solution)/shard_map/all_gather | solution.py:20
  112.5 0.1 broadcast_in_dim.9
  112.7 133.3 %while.29 = (s32[]{:T(128)}, bf16[147,4096]{1,0:T(8,128)(2,1)S(1)}, bf16[440,4096]{1,0:T(8,128)(2,1)}, bf16[440,2048]{1,0:T(8,128)(2,1)}, f32[2048,1]{0,1:T(1,12...) while((s32[]{:T(128)}, bf16[147,4096]{1,0:T(8,128)(2,1)S(1)}, ...), condition=%wide.region_1.0_spmd, body=%wide.region_0.0_spmd.sunk | while | flops 1233125376 | bytes 3196051 | solution.py:46
  112.7 16.6 %fusion.31 = bf16[147,4096]{1,0:T(8,128)(2,1)S(1)} fusion(bf16[147,4096]{1,0:T(8,128)(2,1)S(1)} %get-tuple-element.406, s32[]{:T(128)S(6)} %select_n.20, bf16[147,2048]{1,0:T(8,128)(2,1)S(1)} %get-tuple-element.420, bf16[440,2048]{1,0:T(8,128)(2,1)} %get-tuple-element.418, f32[2048]{0:T(1024)S(1)} %bitcast.32, bf16[440,4096]{1,0:T(8,128)(2,1)} %get-tuple-element.417), kind=kOutput, calls=%fused_computation.2.clone.1 | convolution fusion | flops 1233125376 | bytes 3195904 | tf_op jit(solution)/shard_map/while/body/eval_jaxpr/dot_general | solution.py:43
  129.3 16.6 %fusion.31 = bf16[147,4096]{1,0:T(8,128)(2,1)S(1)} fusion(bf16[147,4096]{1,0:T(8,128)(2,1)S(1)} %get-tuple-element.406, s32[]{:T(128)S(6)} %select_n.20, bf16[147,2048]{1,0:T(8,128)(2,1)S(1)} %get-tuple-element.420, bf16[440,2048]{1,0:T(8,128)(2,1)} %get-tuple-element.418, f32[2048]{0:T(1024)S(1)} %bitcast.32, bf16[440,4096]{1,0:T(8,128)(2,1)} %get-tuple-element.417), kind=kOutput, calls=%fused_computation.2.clone.1 | convolution fusion | flops 1233125376 | bytes 3195904 | tf_op jit(solution)/shard_map/while/body/eval_jaxpr/dot_general | solution.py:43
  146.0 16.6 %fusion.31 = bf16[147,4096]{1,0:T(8,128)(2,1)S(1)} fusion(bf16[147,4096]{1,0:T(8,128)(2,1)S(1)} %get-tuple-element.406, s32[]{:T(128)S(6)} %select_n.20, bf16[147,2048]{1,0:T(8,128)(2,1)S(1)} %get-tuple-element.420, bf16[440,2048]{1,0:T(8,128)(2,1)} %get-tuple-element.418, f32[2048]{0:T(1024)S(1)} %bitcast.32, bf16[440,4096]{1,0:T(8,128)(2,1)} %get-tuple-element.417), kind=kOutput, calls=%fused_computation.2.clone.1 | convolution fusion | flops 1233125376 | bytes 3195904 | tf_op jit(solution)/shard_map/while/body/eval_jaxpr/dot_general | solution.py:43
  162.6 16.6 %fusion.31 = bf16[147,4096]{1,0:T(8,128)(2,1)S(1)} fusion(bf16[147,4096]{1,0:T(8,128)(2,1)S(1)} %get-tuple-element.406, s32[]{:T(128)S(6)} %select_n.20, bf16[147,2048]{1,0:T(8,128)(2,1)S(1)} %get-tuple-element.420, bf16[440,2048]{1,0:T(8,128)(2,1)} %get-tuple-element.418, f32[2048]{0:T(1024)S(1)} %bitcast.32, bf16[440,4096]{1,0:T(8,128)(2,1)} %get-tuple-element.417), kind=kOutput, calls=%fused_computation.2.clone.1 | convolution fusion | flops 1233125376 | bytes 3195904 | tf_op jit(solution)/shard_map/while/body/eval_jaxpr/dot_general | solution.py:43
  179.2 16.6 %fusion.31 = bf16[147,4096]{1,0:T(8,128)(2,1)S(1)} fusion(bf16[147,4096]{1,0:T(8,128)(2,1)S(1)} %get-tuple-element.406, s32[]{:T(128)S(6)} %select_n.20, bf16[147,2048]{1,0:T(8,128)(2,1)S(1)} %get-tuple-element.420, bf16[440,2048]{1,0:T(8,128)(2,1)} %get-tuple-element.418, f32[2048]{0:T(1024)S(1)} %bitcast.32, bf16[440,4096]{1,0:T(8,128)(2,1)} %get-tuple-element.417), kind=kOutput, calls=%fused_computation.2.clone.1 | convolution fusion | flops 1233125376 | bytes 3195904 | tf_op jit(solution)/shard_map/while/body/eval_jaxpr/dot_general | solution.py:43
  195.9 16.6 %fusion.31 = bf16[147,4096]{1,0:T(8,128)(2,1)S(1)} fusion(bf16[147,4096]{1,0:T(8,128)(2,1)S(1)} %get-tuple-element.406, s32[]{:T(128)S(6)} %select_n.20, bf16[147,2048]{1,0:T(8,128)(2,1)S(1)} %get-tuple-element.420, bf16[440,2048]{1,0:T(8,128)(2,1)} %get-tuple-element.418, f32[2048]{0:T(1024)S(1)} %bitcast.32, bf16[440,4096]{1,0:T(8,128)(2,1)} %get-tuple-element.417), kind=kOutput, calls=%fused_computation.2.clone.1 | convolution fusion | flops 1233125376 | bytes 3195904 | tf_op jit(solution)/shard_map/while/body/eval_jaxpr/dot_general | solution.py:43
  212.5 16.6 %fusion.31 = bf16[147,4096]{1,0:T(8,128)(2,1)S(1)} fusion(bf16[147,4096]{1,0:T(8,128)(2,1)S(1)} %get-tuple-element.406, s32[]{:T(128)S(6)} %select_n.20, bf16[147,2048]{1,0:T(8,128)(2,1)S(1)} %get-tuple-element.420, bf16[440,2048]{1,0:T(8,128)(2,1)} %get-tuple-element.418, f32[2048]{0:T(1024)S(1)} %bitcast.32, bf16[440,4096]{1,0:T(8,128)(2,1)} %get-tuple-element.417), kind=kOutput, calls=%fused_computation.2.clone.1 | convolution fusion | flops 1233125376 | bytes 3195904 | tf_op jit(solution)/shard_map/while/body/eval_jaxpr/dot_general | solution.py:43
  229.2 16.6 %fusion.31 = bf16[147,4096]{1,0:T(8,128)(2,1)S(1)} fusion(bf16[147,4096]{1,0:T(8,128)(2,1)S(1)} %get-tuple-element.406, s32[]{:T(128)S(6)} %select_n.20, bf16[147,2048]{1,0:T(8,128)(2,1)S(1)} %get-tuple-element.420, bf16[440,2048]{1,0:T(8,128)(2,1)} %get-tuple-element.418, f32[2048]{0:T(1024)S(1)} %bitcast.32, bf16[440,4096]{1,0:T(8,128)(2,1)} %get-tuple-element.417), kind=kOutput, calls=%fused_computation.2.clone.1 | convolution fusion | flops 1233125376 | bytes 3195904 | tf_op jit(solution)/shard_map/while/body/eval_jaxpr/dot_general | solution.py:43
  246.0 1.0 copy-done.3
  247.0 0.0 all-reduce.2.cloned.1.call-update
  247.0 0.0 all-gather.11.cloned.1.call-start
  247.1 0.7 subtract_convert_fusion
  247.8 0.0 all-gather.11.cloned.1.call-update
  247.8 0.0 reduce-scatter.3.cloned.1.call-start
  247.9 0.0 all-gather.5.cloned.1.call-done
  247.9 119.4 %all-reduce.2.cloned.1.call-done = bf16[147,4096]{1,0:T(8,128)(2,1)} async-done(((bf16[147,4096]{1,0:T(8,128)(2,1)}), bf16[147,4096]{1,0:T(8,128)(2,1)}) %all-reduce.2.cloned.1.call-update) | async-done | bytes 1204240 | tf_op jit(solution)/shard_map/psum | solution.py:47
  367.3 2.1 fusion.12
  369.5 1.4 fusion.11
  370.9 35.0 %all-gather.11.cloned.1.call-done = bf16[147,4096]{1,0:T(8,128)(2,1)} async-done(((bf16[147,256]{1,0:T(8,128)(2,1)}), bf16[147,4096]{1,0:T(8,128)(2,1)}) %all-gather.11.cloned.1.call-update) | async-done | bytes 1204240 | tf_op jit(solution)/shard_map/all_gather | solution.py:21
  405.9 164.4 %while.30 = (s32[]{:T(128)}, f32[147,2048]{1,0:T(8,128)S(1)}, f32[147,2048]{1,0:T(8,128)}, bf16[147,4096]{1,0:T(8,128)(2,1)}, bf16[440,4096]{1,0:T(8,128)(2,1)},...) while((s32[]{:T(128)}, f32[147,2048]{1,0:T(8,128)S(1)}, ...), condition=%wide.region_5.0_spmd.clone, body=%wide.region_4.0_spmd.clone.sunk | while | flops 1542610944 | bytes 13721786 | solution.py:66
  405.9 15.9 %cosine_convert_fusion.3 = bf16[512,2048]{1,0:T(8,128)(2,1)S(1)} fusion(bf16[440,2048]{1,0:T(8,128)(2,1)} %get-tuple-element.454, f32[2048]{0:T(1024)S(1)} %bitcast.33, bf16[440,4096]{1,0:T(8,128)(2,1)} %get-tuple-element.453, s32[]{:T(128)S(6)} %select_n.21), kind=kOutput, calls=%fused_computation.5.clone.1 | convolution fusion | flops 924844032 | bytes 4358148 | tf_op jit(solution)/shard_map/while/body/eval_jaxpr/dot_general | solution.py:32
  421.9 2.6 convolution_add_fusion.5
  424.4 1.6 convolution_add_fusion.4
  426.0 16.0 %cosine_convert_fusion.3 = bf16[512,2048]{1,0:T(8,128)(2,1)S(1)} fusion(bf16[440,2048]{1,0:T(8,128)(2,1)} %get-tuple-element.454, f32[2048]{0:T(1024)S(1)} %bitcast.33, bf16[440,4096]{1,0:T(8,128)(2,1)} %get-tuple-element.453, s32[]{:T(128)S(6)} %select_n.21), kind=kOutput, calls=%fused_computation.5.clone.1 | convolution fusion | flops 924844032 | bytes 4358148 | tf_op jit(solution)/shard_map/while/body/eval_jaxpr/dot_general | solution.py:32
  442.0 3.0 convolution_add_fusion.5
  445.0 1.6 convolution_add_fusion.4
  446.7 16.0 %cosine_convert_fusion.3 = bf16[512,2048]{1,0:T(8,128)(2,1)S(1)} fusion(bf16[440,2048]{1,0:T(8,128)(2,1)} %get-tuple-element.454, f32[2048]{0:T(1024)S(1)} %bitcast.33, bf16[440,4096]{1,0:T(8,128)(2,1)} %get-tuple-element.453, s32[]{:T(128)S(6)} %select_n.21), kind=kOutput, calls=%fused_computation.5.clone.1 | convolution fusion | flops 924844032 | bytes 4358148 | tf_op jit(solution)/shard_map/while/body/eval_jaxpr/dot_general | solution.py:32
  462.6 3.0 convolution_add_fusion.5
  465.7 1.6 convolution_add_fusion.4
  467.3 16.0 %cosine_convert_fusion.3 = bf16[512,2048]{1,0:T(8,128)(2,1)S(1)} fusion(bf16[440,2048]{1,0:T(8,128)(2,1)} %get-tuple-element.454, f32[2048]{0:T(1024)S(1)} %bitcast.33, bf16[440,4096]{1,0:T(8,128)(2,1)} %get-tuple-element.453, s32[]{:T(128)S(6)} %select_n.21), kind=kOutput, calls=%fused_computation.5.clone.1 | convolution fusion | flops 924844032 | bytes 4358148 | tf_op jit(solution)/shard_map/while/body/eval_jaxpr/dot_general | solution.py:32
  483.3 3.0 convolution_add_fusion.5
  486.3 1.6 convolution_add_fusion.4
  487.9 16.0 %cosine_convert_fusion.3 = bf16[512,2048]{1,0:T(8,128)(2,1)S(1)} fusion(bf16[440,2048]{1,0:T(8,128)(2,1)} %get-tuple-element.454, f32[2048]{0:T(1024)S(1)} %bitcast.33, bf16[440,4096]{1,0:T(8,128)(2,1)} %get-tuple-element.453, s32[]{:T(128)S(6)} %select_n.21), kind=kOutput, calls=%fused_computation.5.clone.1 | convolution fusion | flops 924844032 | bytes 4358148 | tf_op jit(solution)/shard_map/while/body/eval_jaxpr/dot_general | solution.py:32
  503.9 3.0 convolution_add_fusion.5
  506.9 1.6 convolution_add_fusion.4
  508.5 16.0 %cosine_convert_fusion.3 = bf16[512,2048]{1,0:T(8,128)(2,1)S(1)} fusion(bf16[440,2048]{1,0:T(8,128)(2,1)} %get-tuple-element.454, f32[2048]{0:T(1024)S(1)} %bitcast.33, bf16[440,4096]{1,0:T(8,128)(2,1)} %get-tuple-element.453, s32[]{:T(128)S(6)} %select_n.21), kind=kOutput, calls=%fused_computation.5.clone.1 | convolution fusion | flops 924844032 | bytes 4358148 | tf_op jit(solution)/shard_map/while/body/eval_jaxpr/dot_general | solution.py:32
  524.5 3.0 convolution_add_fusion.5
  527.5 1.6 convolution_add_fusion.4
  529.1 16.0 %cosine_convert_fusion.3 = bf16[512,2048]{1,0:T(8,128)(2,1)S(1)} fusion(bf16[440,2048]{1,0:T(8,128)(2,1)} %get-tuple-element.454, f32[2048]{0:T(1024)S(1)} %bitcast.33, bf16[440,4096]{1,0:T(8,128)(2,1)} %get-tuple-element.453, s32[]{:T(128)S(6)} %select_n.21), kind=kOutput, calls=%fused_computation.5.clone.1 | convolution fusion | flops 924844032 | bytes 4358148 | tf_op jit(solution)/shard_map/while/body/eval_jaxpr/dot_general | solution.py:32
  545.1 3.0 convolution_add_fusion.5
  548.1 1.6 convolution_add_fusion.4
  549.7 16.0 %cosine_convert_fusion.3 = bf16[512,2048]{1,0:T(8,128)(2,1)S(1)} fusion(bf16[440,2048]{1,0:T(8,128)(2,1)} %get-tuple-element.454, f32[2048]{0:T(1024)S(1)} %bitcast.33, bf16[440,4096]{1,0:T(8,128)(2,1)} %get-tuple-element.453, s32[]{:T(128)S(6)} %select_n.21), kind=kOutput, calls=%fused_computation.5.clone.1 | convolution fusion | flops 924844032 | bytes 4358148 | tf_op jit(solution)/shard_map/while/body/eval_jaxpr/dot_general | solution.py:32
  565.7 3.0 convolution_add_fusion.5
  568.7 1.6 convolution_add_fusion.4
  570.4 1.0 copy-done
  571.4 0.0 reduce-scatter.3.cloned.1.call-update
  571.4 0.0 reduce-scatter.5.cloned.1.call-start
  571.5 0.7 reduce-scatter.5.cloned.1.call-update
  572.8 70.9 %reduce-scatter.3.cloned.1.call-done = f32[147,256]{1,0:T(8,128)} async-done(((f32[147,2048]{1,0:T(8,128)}), f32[147,256]{1,0:T(8,128)}) %reduce-scatter.3.cloned.1.call-update) | async-done | bytes 150544 | tf_op jit(solution)/shard_map/reduce_scatter | solution.py:68
  643.7 1.6 multiply_add_fusion
  645.3 75.7 %reduce-scatter.5.cloned.1.call-done = f32[147,256]{1,0:T(8,128)} async-done(((f32[147,2048]{1,0:T(8,128)}), f32[147,256]{1,0:T(8,128)}) %reduce-scatter.5.cloned.1.call-update) | async-done | bytes 150544 | tf_op jit(solution)/shard_map/reduce_scatter | solution.py:69
  (15 shorter events, 0.0 us)
Async XLA Ops:
  7.2 61.5 %all-gather.9.cloned.1.call-start = ((), (), s32[]{:S(2)}) async-start(), calls=%async_computation.4 | async-start | bytes 2027520 | tf_op jit(solution)/shard_map/all_gather | solution.py:14
  7.9 104.6 %all-gather.7.cloned.1.call-start = ((), (), s32[]{:S(2)}) async-start(), calls=%async_computation.3 | async-start | bytes 3829760 | tf_op jit(solution)/shard_map/all_gather | solution.py:20
  8.6 239.2 %all-gather.5.cloned.1.call-start = ((), (), s32[]{:S(2)}) async-start(), calls=%async_computation.2 | async-start | bytes 1323008 | tf_op jit(solution)/shard_map/all_gather | solution.py:22
  9.4 358.0 %all-reduce.2.cloned.1.call-start = ((), (), s32[]{:S(2)}) async-start(), calls=%async_computation.5 | async-start | bytes 2490368 | tf_op jit(solution)/shard_map/psum | solution.py:47
  112.6 134.5 %copy-start.4 = (bf16[147,256]{1,0:T(8,128)(2,1)S(1)}, bf16[147,256]{1,0:T(8,128)(2,1)}, u32[]{:S(2)}) copy-start(bf16[147,256]{1,0:T(8,128)(2,1)} %param.12) | copy-start | bytes 225796
  112.6 134.5 %copy-start.6 = (s32[256]{0:T(256)S(1)}, s32[256]{0:T(256)}, u32[]{:S(2)}) copy-start(s32[256]{0:T(256)} %param.13) | copy-start | bytes 3076
  246.0 1.1 copy-start.3
  247.0 158.9 %all-gather.11.cloned.1.call-start = ((), (), s32[]{:S(2)}) async-start(), calls=%async_computation.6 | async-start | bytes 1323008 | tf_op jit(solution)/shard_map/all_gather | solution.py:21
  247.8 395.9 %reduce-scatter.3.cloned.1.call-start = ((), (), s32[]{:S(2)}) async-start(), calls=%async_computation.7 | async-start | bytes 1400832 | tf_op jit(solution)/shard_map/reduce_scatter | solution.py:68
  247.9 121.6 %copy-start.1 = (bf16[147,4096]{1,0:T(8,128)(2,1)S(1)}, bf16[147,4096]{1,0:T(8,128)(2,1)}, u32[]{:S(2)}) copy-start(bf16[147,4096]{1,0:T(8,128)(2,1)} %all-gather.5.cloned.1.call-done) | copy-start | bytes 3612676
  367.3 2.1 copy-start.2
  570.3 1.1 copy-start
  570.3 73.4 %copy-start.5 = (bf16[147,256]{1,0:T(8,128)(2,1)S(1)}, bf16[147,256]{1,0:T(8,128)(2,1)}, u32[]{:S(2)}) copy-start(bf16[147,256]{1,0:T(8,128)(2,1)} %param.16) | copy-start | bytes 225796
  571.4 149.6 %reduce-scatter.5.cloned.1.call-start = ((), (), s32[]{:S(2)}) async-start(), calls=%async_computation.8 | async-start | bytes 1400832 | tf_op jit(solution)/shard_map/reduce_scatter | solution.py:69
Sparse Core Ops, SparseCore 0:
  10.2 58.4 all-gather.8
  70.3 42.1 all-gather.6
  114.1 34.6 all-gather.4
  247.2 120.1 all-reduce.1
  369.4 36.5 all-gather.10
  571.5 72.1 reduce-scatter.2
  647.9 73.0 reduce-scatter.4
where the time goes:
time: 730 us; the launch traced here: 728 us
  waiting for transfers between devices  350 us (48%)
  matrix products  297 us (41%)
  blocking collectives  56.4 us (8%)
  between operations  14.9 us (2%)
    dot_general x8, matrix products, first_late(): piece = jnp.dot(dir_all, feats, preferred_element_type=jnp.float32)  133 us
    dot_general x8, matrix products, features(): lax.dot_general(w_all, x_block, (((0,), (0,)), ((), ())), preferred_eleme...  128 us
    psum x1, waiting for transfers between devices, on_device(): total = lax.psum(tangent.astype(jnp.bfloat16), 'feat').astype(jnp.float32)  119 us
    reduce_scatter x1, waiting for transfers between devices, on_device(): lax.psum_scatter(grad_acc, 'samp', scatter_dimension=1, tiled=True)  75.7 us
    reduce_scatter x1, waiting for transfers between devices, on_device(): lax.psum_scatter(hv_acc, 'samp', scatter_dimension=1, tiled=True)  70.9 us
    all_gather x1, waiting for transfers between devices, on_device(): lax.all_gather(inputs, 'feat', axis=1, tiled=True)  43.8 us
    all_gather x1, waiting for transfers between devices, on_device(): lax.all_gather(own_resid, 'feat', axis=1, tiled=True)  35 us
    all_gather x1, blocking collectives, on_device(): lax.all_gather(direction, 'samp', axis=1, tiled=True)  34.2 us
  transfers between devices with their start and end apart: 7, of which 6 were waited for; matrix products, arithmetic and copies ran while one was open for 19% of the time, Pallas kernels for 0%

commit v1 on v0

v1 whole, which is shorter than its diff:
```python
import math

import jax
import jax.numpy as jnp
from jax import lax
from jax.experimental import pallas as pl
from jax.experimental.pallas import tpu as pltpu
from jax.sharding import PartitionSpec as P

MESH = pl.DeviceIdType.MESH
BF = jnp.bfloat16
F32 = jnp.float32
TURN = 1.0 / (2.0 * math.pi)
SINE = (6.283185160088606, -41.34165503119389, 81.60100405839074, -76.54978193238271, 39.536703184435794)

RAWP = 448
CP = 160
WROWS = RAWP + CP
KX = 512

XQ = ((0, 0), (3, 0), (1, 0), (0, 1), (2, 0), (3, 1), (1, 1), (2, 1))
WQ = ((0, 0), (3, 0), (1, 0), (0, 1), (2, 0), (3, 1), (1, 1), (2, 1))
XS = tuple((dx, dy, dc) for dx, dy in XQ for dc in (0, 1))


def xslot(dx, dy, dc):
    return XS.index((dx % 4, dy % 2, dc % 2))


def wslot(dz, dy):
    return WQ.index((dz % 4, dy % 2))


def cosine(u):
    t = u * TURN
    y = 0.25 - jnp.abs(t - jnp.round(t))
    z = y * y
    p = F32(SINE[-1])
    for c in SINE[-2::-1]:
        p = p * z + F32(c)
    return (p * y).astype(BF)


def kernel(x_ref, prob_ref, lab_ref, w_ref, ph_ref, dir_ref, damp_ref, hess_ref, grad_ref,
           xg, wg, feats, dirb, tsend, trecv, resid, curv, gsend, grecv, hsend, hrecv,
           loc_sem, xs_sem, xr_sem, ws_sem, wr_sem, ts_sem, tr_sem, rs_sem, rr_sem,
           cs_sem, cr_sem, gs_sem, gr_sem, hs_sem, hr_sem):
    samp = lax.axis_index("samp")
    feat = lax.axis_index("feat")
    z, yh = samp // 2, samp % 2
    yl, x, core = feat // 8, (feat // 2) % 4, feat % 2

    def dev(dx=0, dyl=0, dc=0, dz=0, dyh=0):
        s = ((z + dz) % 4) * 2 + (yh + dyh) % 2
        f = (((yl + dyl) % 2) * 4 + (x + dx) % 4) * 2 + (core + dc) % 2
        return (s, f)

    barrier = pltpu.get_barrier_semaphore()
    for dx, dy, dc in XS[1:]:
        pl.semaphore_signal(barrier, inc=1, device_id=dev(dx=dx, dyl=dy, dc=dc), device_id_type=MESH)
    for dz, dy in WQ[1:]:
        pl.semaphore_signal(barrier, inc=1, device_id=dev(dz=dz, dyh=dy), device_id_type=MESH)

    wv = jnp.concatenate(
        [w_ref[...].astype(F32),
         jnp.where(lax.broadcasted_iota(jnp.int32, (8, 256), 0) == 0, ph_ref[...].astype(F32), 0.0)], axis=0)
    wg[0, 0:RAWP, :] = wv.astype(BF)
    wg[0, WROWS - 16:WROWS, :] = jnp.zeros((16, 256), BF)
    wg[0, RAWP:RAWP + 147, :] = dir_ref[...]
    xv = jnp.concatenate(
        [x_ref[...].astype(F32),
         jnp.where(lax.broadcasted_iota(jnp.int32, (KX - 440, 256), 0) == 0, 1.0, 0.0)], axis=0)
    xg[0] = xv.T.astype(BF)
    prob = prob_ref[...].astype(F32)
    onehot = (lax.broadcasted_iota(jnp.int32, (147, 256), 0) == lab_ref[...]).astype(F32)
    resid[CP - 16:CP, 0:256] = jnp.zeros((16, 256), BF)
    resid[0:147, 0:256] = (prob - onehot).astype(BF)

    pl.semaphore_wait(barrier, 22)

    sends = []

    def put(src, dst, ssem, rsem, target):
        c = pltpu.make_async_remote_copy(
            src_ref=src, dst_ref=dst, send_sem=ssem, recv_sem=rsem, device_id=target, device_id_type=MESH)
        c.start()
        sends.append(c)

    nx = [0]
    nw = [0]

    def xput(frm, to, target, half=None):
        k = nx[0]
        nx[0] += 1
        if half is None:
            put(xg.at[frm], xg.at[to], xs_sem.at[k], xr_sem.at[to, 0], target)
        else:
            rows = pl.ds(half * 128, 128)
            put(xg.at[frm, rows], xg.at[to, rows], xs_sem.at[k], xr_sem.at[to, half], target)

    def wput(frm, to, target, half=None):
        k = nw[0]
        nw[0] += 1
        if half is None:
            put(wg.at[frm], wg.at[to], ws_sem.at[k], wr_sem.at[to, 0], target)
        else:
            rows = pl.ds(half * (WROWS // 2), WROWS // 2)
            put(wg.at[frm, rows], wg.at[to, rows], ws_sem.at[k], wr_sem.at[to, half], target)

    def wait_in(ref, sem):
        pltpu.make_async_copy(ref, ref, sem).wait()

    def xwait(k):
        dx, dy, dc = XS[k]
        if dx == 2 and dc == 0:
            for h in (0, 1):
                rows = pl.ds(h * 128, 128)
                wait_in(xg.at[k, rows], xr_sem.at[k, h])
        else:
            wait_in(xg.at[k], xr_sem.at[k, 0])

    def wwait(k):
        dz, dy = WQ[k]
        if dz == 2:
            for h in (0, 1):
                rows = pl.ds(h * (WROWS // 2), WROWS // 2)
                wait_in(wg.at[k, rows], wr_sem.at[k, h])
        else:
            wait_in(wg.at[k], wr_sem.at[k, 0])

    xp, xm = dev(dx=1), dev(dx=3)
    zp, zm = dev(dz=1), dev(dz=3)
    sib = dev(dc=1)

    wput(0, wslot(3, 0), zp)
    wput(0, wslot(1, 0), zm)
    wput(0, wslot(0, 1), dev(dyh=1))
    xput(0, xslot(3, 0, 0), xp)
    xput(0, xslot(1, 0, 0), xm)
    xput(0, xslot(0, 1, 0), dev(dyl=1))
    xput(0, xslot(0, 0, 1), sib)

    def wfwd(k):
        wwait(k)
        dz, dy = WQ[k]
        if dz == 0:
            wput(k, wslot(3, dy), zp)
            wput(k, wslot(1, dy), zm)
        elif dz == 3:
            wput(k, wslot(2, dy), zp, 0)
        elif dz == 1:
            wput(k, wslot(2, dy), zm, 1)

    def xfwd(k):
        xwait(k)
        dx, dy, dc = XS[k]
        if dx == 0:
            xput(k, xslot(3, dy, 0), xp)
            xput(k, xslot(1, dy, 0), xm)
        elif dx == 3:
            xput(k, xslot(2, dy, 0), xp, 0)
        elif dx == 1:
            xput(k, xslot(2, dy, 0), xm, 1)
        xput(k, xslot(dx, dy, 1), sib)

    for q in range(1, 8):
        wfwd(q)
        xfwd(2 * q)

    for j in range(8):
        dirb[:, j * 256:(j + 1) * 256] = wg[j, RAWP:WROWS, :]
    for q in range(8):
        xwait(2 * q + 1)

    def spread(buf, s_sem, r_sem):
        for i, (dx, dy) in enumerate(XQ[1:]):
            to = xslot(-dx, dy, 0)
            put(buf.at[:, pl.ds(0, 256)], buf.at[:, pl.ds(to * 256, 256)],
                s_sem.at[i], r_sem.at[to], dev(dx=dx, dyl=dy))
        to = xslot(0, 0, 1)
        put(buf.at[:, pl.ds(0, 256)], buf.at[:, pl.ds(to * 256, 256)], s_sem.at[7], r_sem.at[to], sib)

    def relay(buf, s_sem, r_sem):
        for i, (dx, dy) in enumerate(XQ[1:]):
            k, to = xslot(dx, dy, 0), xslot(dx, dy, 1)
            wait_in(buf.at[:, pl.ds(k * 256, 256)], r_sem.at[k])
            put(buf.at[:, pl.ds(k * 256, 256)], buf.at[:, pl.ds(to * 256, 256)],
                s_sem.at[8 + i], r_sem.at[to], sib)
        for dx, dy in XQ:
            k = xslot(dx, dy, 1)
            wait_in(buf.at[:, pl.ds(k * 256, 256)], r_sem.at[k])

    spread(resid, rs_sem, rr_sem)

    def tcopy(k):
        dx, dy, dc = XS[k]
        to = xslot(-dx, dy, dc)
        return pltpu.make_async_remote_copy(
            src_ref=tsend.at[k], dst_ref=trecv.at[to], send_sem=ts_sem.at[k], recv_sem=tr_sem.at[to],
            device_id=dev(dx=dx, dyl=dy, dc=dc), device_id_type=MESH)

    def shard(step, carry):
        i = 15 - step
        rows = pl.ds(pl.multiple_of(i * 256, 256), 256)
        xv = xg[i]
        for j in range(8):
            u = jnp.dot(xv, wg[j, 0:KX, :], preferred_element_type=F32)
            feats[rows, j * 256:(j + 1) * 256] = cosine(u)
        t = lax.dot_general(feats[rows, :], dirb[...], (((1,), (1,)), ((), ())), preferred_element_type=F32)
        tsend[i] = t.T.astype(BF)
        for k in range(1, 16):
            @pl.when(i == k)
            def _():
                tcopy(k).start()
        return carry

    lax.fori_loop(0, 16, shard, 0)
    relay(resid, rs_sem, rr_sem)

    total = tsend[0].astype(F32)
    for k in range(1, 16):
        wait_in(trecv.at[k], tr_sem.at[k])
        total = total + trecv[k].astype(F32)
    total = total[0:147]
    mixed = jnp.sum(prob * total, axis=0, keepdims=True)
    curv[CP - 16:CP, 0:256] = jnp.zeros((16, 256), BF)
    curv[0:147, 0:256] = (prob * (total - mixed)).astype(BF)
    spread(curv, cs_sem, cr_sem)

    def share(buf, own, send, recv, s_sem, r_sem):
        for j in (7, 5, 6, 4, 3, 1, 2, 0):
            v = jnp.dot(buf[...], feats[:, j * 256:(j + 1) * 256], preferred_element_type=F32)
            if j == 0:
                own[...] = v[0:147]
            else:
                dz, dy = WQ[j]
                to = wslot(-dz, dy)
                send[j] = v.astype(BF)
                put(send.at[j], recv.at[to], s_sem.at[j], r_sem.at[to], dev(dz=dz, dyh=dy))

    share(resid, grad_ref, gsend, grecv, gs_sem, gr_sem)
    relay(curv, cs_sem, cr_sem)
    share(curv, hess_ref, hsend, hrecv, hs_sem, hr_sem)

    g = grad_ref[...]
    for k in range(1, 8):
        wait_in(grecv.at[k], gr_sem.at[k])
        g = g + grecv[k].astype(F32)[0:147]
    grad_ref[...] = g
    h = hess_ref[...] + damp_ref[0] * dir_ref[...].astype(F32)
    for k in range(1, 8):
        wait_in(hrecv.at[k], hr_sem.at[k])
        h = h + hrecv[k].astype(F32)[0:147]
    hess_ref[...] = h

    for c in sends:
        c.wait_send()
    for k in range(1, 16):
        tcopy(k).wait_send()


def on_device(inputs, probs, labels, proj_weight, phase, direction, damping):
    vmem = pl.BlockSpec(memory_space=pltpu.VMEM)
    dma = pltpu.SemaphoreType.DMA
    out = jax.ShapeDtypeStruct(direction.shape, F32)
    return pl.pallas_call(
        kernel,
        out_shape=(out, out),
        in_specs=[vmem] * 6 + [pl.BlockSpec(memory_space=pltpu.SMEM)],
        out_specs=(vmem, vmem),
        scratch_shapes=[
            pltpu.VMEM((16, 256, KX), BF),
            pltpu.VMEM((8, WROWS, 256), BF),
            pltpu.VMEM((4096, 2048), BF),
            pltpu.VMEM((CP, 2048), BF),
            pltpu.VMEM((16, CP, 256), BF),
            pltpu.VMEM((16, CP, 256), BF),
            pltpu.VMEM((CP, 4096), BF),
            pltpu.VMEM((CP, 4096), BF),
            pltpu.VMEM((8, CP, 256), BF),
            pltpu.VMEM((8, CP, 256), BF),
            pltpu.VMEM((8, CP, 256), BF),
            pltpu.VMEM((8, CP, 256), BF),
            dma((1,)), dma((20,)), dma((16, 2)), dma((12,)), dma((8, 2)),
            dma((16,)), dma((16,)), dma((16,)), dma((16,)),
            dma((16,)), dma((16,)), dma((8,)), dma((8,)), dma((8,)), dma((8,)),
        ],
        compiler_params=pltpu.CompilerParams(
            collective_id=0, has_side_effects=True, vmem_limit_bytes=56 * 1024 * 1024),
    )(inputs, probs, labels.reshape(1, -1), proj_weight, phase, direction, damping)


def solution(mesh):
    placed = (
        P(None, ("samp", "feat")),
        P(None, ("samp", "feat")),
        P(("samp", "feat")),
        P(None, ("feat", "samp")),
        P(None, ("feat", "samp")),
        P(None, ("feat", "samp")),
        P(),
    )
    return jax.shard_map(
        on_device,
        mesh=mesh,
        in_specs=placed,
        out_specs=(P(None, ("feat", "samp")), P(None, ("feat", "samp"))),
        check_vma=False,
    )
```

time: 730 us -> 94.4 us (0.13)
  waiting for transfers between devices: 350 us -> 0 us
  matrix products: 297 us -> 0 us
  Pallas kernels: 0 us -> 90.7 us
  blocking collectives: 56.4 us -> 0 us
  between operations: 14.9 us -> 1.3 us
    dot_general x32 -> x0, matrix products: 297 us -> none  [the longest x8 133 us: first_late(): piece = jnp.dot(dir_all, feats, preferred_element_type=jnp.float32)]
    reduce_scatter x2 -> x0, waiting for transfers between devices: 147 us -> none  [the longest x1 75.7 us: on_device(): lax.psum_scatter(grad_acc, 'samp', scatter_dimension=1, tiled=True)]
    psum x1 -> x0, waiting for transfers between devices: 119 us -> none  [on_device(): total = lax.psum(tangent.astype(jnp.bfloat16), 'feat').astype(jnp.float32)]
    pallas_call x0 -> x1, Pallas kernels: none -> 90.7 us  [on_device(): pl.pallas_call(kernel, out_shape=(out, out), in_specs=[vmem] * 6 + [pl.Bl...]
    all_gather x4 -> x0, waiting for transfers between devices: 81.6 us -> none  [the longest x1 43.8 us: on_device(): lax.all_gather(inputs, 'feat', axis=1, tiled=True)]
    all_gather x2 -> x0, blocking collectives: 56.4 us -> none  [the longest x1 34.2 us: on_device(): lax.all_gather(direction, 'samp', axis=1, tiled=True)]
  transfers between devices with their start and end apart: 7 -> 0, of which waited for: 6 -> 0; matrix products, arithmetic and copies ran while one was open for 19% -> 0% of each run, Pallas kernels for 0% -> 0%
where the time goes in v1:
time: 94.4 us; the launch traced here: 94.3 us
  Pallas kernels  90.7 us (96%)
  local copies, waits for them, and re-layouts  2.29 us (2%)
  between operations  1.3 us (1%)
    pallas_call x1, Pallas kernels, on_device(): pl.pallas_call(kernel, out_shape=(out, out), in_specs=[vmem] * 6 + [pl.Bl...  90.7 us
    unnamed x4, local copies, waits for them, and re-layouts  2.29 us

profile of v1, /device:TPU:1, one launch (start us, length us, event | category | flops | bytes accessed | tf_op | source)
XLA Modules:
  0.0 94.3 jit_solution(8527629112087091859)
XLA Ops:
  1.3 90.7 %shard_map.86 = (f32[147,256]{1,0:T(8,128)}, f32[147,256]{1,0:T(8,128)}) custom-call(bf16[440,256]{1,0:T(8,128)(2,1)} %x_ref.1, bf16[147,256]{1,0:T(8,128)(2,1)} %prob_ref.1, s32[1,256]{1,0:T(1,128)} %bitcast.1, bf16[440,256]{1,0:T(8,128)(2,1)} %w_ref.1, bf16[1,256]{1,0:T(2,128)(2,1)} %ph_ref.1, bf16[147,256]{1,0:T(8,128)(2,1)} %dir_ref.1, f32[1]{0:T(128)S(6)} %copy.11.damp_ref), custom_call_target="tpu_custom_call" | custom-call | tf_op jit(solution)/shard_map/pallas_call | solution.py:266
  92.0 0.0 copy-start
  92.0 1.6 %copy.12 = f32[147,256]{1,0:T(8,128)} copy(f32[147,256]{1,0:T(8,128)} %get-tuple-element.4) | data formatting | bytes 301056
  93.6 0.0 copy-done
  93.6 0.7 copy.13
Async XLA Ops:
  92.0 1.6 %copy-start = (f32[147,256]{1,0:T(8,128)S(1)}, f32[147,256]{1,0:T(8,128)}, u32[]{:S(2)}) copy-start(f32[147,256]{1,0:T(8,128)} %get-tuple-element.5) | copy-start | bytes 451588

commit v2 on v0

v2 whole, which is shorter than its diff:
```python
import math

import jax
import jax.numpy as jnp
from jax import lax
from jax.experimental import pallas as pl
from jax.experimental.pallas import tpu as pltpu
from jax.sharding import PartitionSpec as P

MESH = pl.DeviceIdType.MESH
BF = jnp.bfloat16
F32 = jnp.float32
TURN = 1.0 / (2.0 * math.pi)
SINE = (6.283185160088606, -41.34165503119389, 81.60100405839074, -76.54978193238271, 39.536703184435794)

RAWP = 448
CP = 160
KX = 512
HALF = 128
WH = RAWP // 2

RING = ((0, 0), (3, 0), (1, 0), (2, 0), (0, 1), (3, 1), (1, 1), (2, 1))


def chip(a, b):
    return RING.index((a % 4, b % 2))


def cosine(u):
    t = u * TURN
    y = 0.25 - jnp.abs(t - jnp.round(t))
    z = y * y
    p = F32(SINE[-1])
    for c in SINE[-2::-1]:
        p = p * z + F32(c)
    return (p * y).astype(BF)


def kernel(x_ref, prob_ref, lab_ref, w_ref, ph_ref, dir_ref, damp_ref, hess_ref, grad_ref,
           xg, wg, fa, fb, dirg, dirt, tkeep, tss, tsr, tse, trecv, resid, curv,
           gsend, grecv, hsend, hrecv, hacc, gkeep,
           xs_sem, xr_sem, ws_sem, wr_sem, ds_sem, dr_sem, bs_sem, br_sem, ts_sem, tr_sem,
           rs_sem, rr_sem, cs_sem, cr_sem, gs_sem, gr_sem, hs_sem, hr_sem):
    samp = lax.axis_index("samp")
    feat = lax.axis_index("feat")
    z, yh = samp // 2, samp % 2
    yl, x, core = feat // 8, (feat // 2) % 4, feat % 2

    def dev(dx=0, dyl=0, dc=0, dz=0, dyh=0):
        s = ((z + dz) % 4) * 2 + (yh + dyh) % 2
        f = (((yl + dyl) % 2) * 4 + (x + dx) % 4) * 2 + (core + dc) % 2
        return (s, f)

    xp, xm, x2, yp = dev(dx=1), dev(dx=3), dev(dx=2), dev(dyl=1)
    zp, zm, z2, yq = dev(dz=1), dev(dz=3), dev(dz=2), dev(dyh=1)
    sib = dev(dc=1)

    barrier = pltpu.get_barrier_semaphore()
    greet = [sib] + [dev(dx=a, dyl=b) for a, b in RING[1:]] + [dev(dz=a, dyh=b) for a, b in RING[1:]]
    for d in greet:
        pl.semaphore_signal(barrier, inc=1, device_id=d, device_id_type=MESH)

    wv = jnp.concatenate(
        [w_ref[...].astype(F32),
         jnp.where(lax.broadcasted_iota(jnp.int32, (8, 256), 0) == 0, ph_ref[...].astype(F32), 0.0)], axis=0)
    wg[0, 0:RAWP, :] = wv.astype(BF)
    for j in range(8):
        wg[j, RAWP:KX, :] = jnp.zeros((KX - RAWP, 256), BF)
    xv = jnp.concatenate(
        [x_ref[...].astype(F32),
         jnp.where(lax.broadcasted_iota(jnp.int32, (KX - 440, 256), 0) == 0, 1.0, 0.0)], axis=0)
    xt = xv.T.astype(BF)
    xg[0, 0] = xt[0:HALF]
    xg[1, 0] = xt[HALF:]
    dirg[0, CP - 16:CP, :] = jnp.zeros((16, 256), BF)
    dirg[0, 0:147, :] = dir_ref[...]
    prob = prob_ref[...].astype(F32)
    onehot = (lax.broadcasted_iota(jnp.int32, (147, 256), 0) == lab_ref[...]).astype(F32)
    own_resid = (prob - onehot).astype(BF)
    for p in (0, 1):
        lanes = slice(p * 2048, p * 2048 + HALF)
        resid[CP - 16:CP, lanes] = jnp.zeros((16, HALF), BF)
        resid[0:147, lanes] = own_resid[:, p * HALF:(p + 1) * HALF]
        curv[CP - 16:CP, lanes] = jnp.zeros((16, HALF), BF)

    pl.semaphore_wait(barrier, len(greet))

    sends = []
    used = {}

    def put(src, dst, ssems, rsem, target):
        k = used.get(id(ssems), 0)
        used[id(ssems)] = k + 1
        c = pltpu.make_async_remote_copy(
            src_ref=src, dst_ref=dst, send_sem=ssems.at[k], recv_sem=rsem, device_id=target, device_id_type=MESH)
        c.start()
        sends.append(c)

    def wait_in(ref, sem):
        pltpu.make_async_copy(ref, ref, sem).wait()

    def wput(frm, to, target, h):
        rows = pl.ds(h * WH, WH)
        put(wg.at[frm, rows], wg.at[to, rows], ws_sem, wr_sem.at[to, h], target)

    def wwait(k, h):
        wait_in(wg.at[k, pl.ds(h * WH, WH)], wr_sem.at[k, h])

    def wturn(b, h):
        k = chip(3 if h == 0 else 1, b)
        wwait(k, h)
        wput(k, chip(2, b), zp if h == 0 else zm, h)

    def xput(p, frm, to, target, h=None):
        if h is None:
            put(xg.at[p, frm], xg.at[p, to], xs_sem, xr_sem.at[p, to, 0], target)
        else:
            rows = pl.ds(h * (HALF // 2), HALF // 2)
            put(xg.at[p, frm, rows], xg.at[p, to, rows], xs_sem, xr_sem.at[p, to, h], target)

    def xwait(p, q):
        if RING[q][0] == 2:
            for h in (0, 1):
                rows = pl.ds(h * (HALF // 2), HALF // 2)
                wait_in(xg.at[p, 2 * q, rows], xr_sem.at[p, 2 * q, h])
        else:
            wait_in(xg.at[p, 2 * q], xr_sem.at[p, 2 * q, 0])

    def xfwd(p, q):
        a, b = RING[q]
        xwait(p, q)
        if a == 0:
            xput(p, 2 * q, 2 * chip(3, b), xp)
            xput(p, 2 * q, 2 * chip(1, b), xm)
        elif a == 3:
            xput(p, 2 * q, 2 * chip(2, b), xp, 0)
        elif a == 1:
            xput(p, 2 * q, 2 * chip(2, b), xm, 1)
        xput(p, 2 * q, 2 * q + 1, sib)

    def xsib(p, qs):
        for q in qs:
            wait_in(xg.at[p, 2 * q + 1], xr_sem.at[p, 2 * q + 1, 0])

    def xown(p):
        xput(p, 0, 2 * chip(3, 0), xp)
        xput(p, 0, 2 * chip(1, 0), xm)
        xput(p, 0, 2 * chip(0, 1), yp)

    def lanes_of(p, k):
        return pl.ds(p * 2048 + k * HALF, HALF)

    def bput(buf, p, frm, to, s_sem, r_sem, target):
        put(buf.at[:, lanes_of(p, frm)], buf.at[:, lanes_of(p, to)], s_sem, r_sem.at[p, to], target)

    def bwait(buf, p, k, r_sem):
        wait_in(buf.at[:, lanes_of(p, k)], r_sem.at[p, k])

    def spread0(buf, p, s_sem, r_sem):
        bput(buf, p, 0, 2 * chip(0, 1), s_sem, r_sem, yp)
        bput(buf, p, 0, 2 * chip(2, 0), s_sem, r_sem, x2)
        bput(buf, p, 0, 2 * chip(3, 0), s_sem, r_sem, xp)
        bput(buf, p, 0, 2 * chip(1, 0), s_sem, r_sem, xm)
        bput(buf, p, 0, 1, s_sem, r_sem, sib)

    def spread1(buf, p, s_sem, r_sem):
        k = 2 * chip(0, 1)
        bwait(buf, p, k, r_sem)
        bput(buf, p, k, 2 * chip(2, 1), s_sem, r_sem, x2)
        bput(buf, p, k, 2 * chip(3, 1), s_sem, r_sem, xp)
        bput(buf, p, k, 2 * chip(1, 1), s_sem, r_sem, xm)
        bput(buf, p, k, k + 1, s_sem, r_sem, sib)

    def spread2(buf, p, b, s_sem, r_sem):
        for a in (3, 1, 2):
            k = 2 * chip(a, b)
            bwait(buf, p, k, r_sem)
            bput(buf, p, k, k + 1, s_sem, r_sem, sib)

    def spread3(buf, p, r_sem):
        for q in range(8):
            bwait(buf, p, 2 * q + 1, r_sem)

    RES = (rs_sem, rr_sem)
    CUR = (cs_sem, cr_sem)

    feats = (fa, fb)

    def block(p, q, j0, j1):
        rows = pl.ds(pl.multiple_of(q * 256, 256), 256)
        v = xg[p, pl.ds(2 * q, 2)].reshape(256, KX)
        for j in range(j0, j1):
            u = jnp.dot(v, wg[j], preferred_element_type=F32)
            feats[p][rows, j * 256:(j + 1) * 256] = cosine(u)

    def blocks(p, q0, q1, j0, j1):
        def step(i, carry):
            block(p, q0 + 2 * i, j0, j1)
            block(p, q0 + 2 * i + 1, j0, j1)
            return carry
        lax.fori_loop(0, (q1 - q0) // 2, step, 0)

    def tdot(p, q, n=2):
        return jnp.dot(feats[p][q * 256:(q + n) * 256, :], dirt[...], preferred_element_type=F32)

    def tput(p, q, t, n=2):
        tt = t.T
        for i in range(n):
            tkeep[p, q + i] = tt[:, i * 256:i * 256 + HALF]
            tss[p, q + i] = tt[:, i * 256 + HALF:i * 256 + 256].astype(BF)
            put(tss.at[p, q + i], tsr.at[p, q + i], bs_sem, br_sem.at[p, q + i], sib)

    def tsum(p, q):
        wait_in(tsr.at[p, q], br_sem.at[p, q])
        c = tkeep[p, q] + tsr[p, q].astype(F32)
        if q == 0:
            tkeep[p, 0] = c
        else:
            a, b = RING[q]
            to = chip(-a, b)
            tse[p, q] = c.astype(BF)
            put(tse.at[p, q], trecv.at[p, to], ts_sem, tr_sem.at[p, to], dev(dx=a, dyl=b))

    def curvature(p):
        total = tkeep[p, 0]
        for k in range(1, 8):
            wait_in(trecv.at[p, k], tr_sem.at[p, k])
            total = total + trecv[p, k].astype(F32)
        total = total[0:147]
        pr = prob_ref[:, p * HALF:(p + 1) * HALF].astype(F32)
        mixed = jnp.sum(pr * total, axis=0, keepdims=True)
        curv[0:147, p * 2048:p * 2048 + HALF] = (pr * (total - mixed)).astype(BF)
        spread0(curv, p, *CUR)

    wput(0, chip(3, 0), zp, 0)
    wput(0, chip(1, 0), zm, 1)
    wput(0, chip(0, 1), yq, 0)
    xown(0)
    wput(0, chip(3, 0), zp, 1)
    wput(0, chip(1, 0), zm, 0)
    wput(0, chip(0, 1), yq, 1)
    xput(0, 0, 1, sib)
    xput(1, 0, 1, sib)

    def dput(frm, to, target):
        put(dirg.at[frm], dirg.at[to], ds_sem, dr_sem.at[to], target)

    dput(0, chip(0, 1), yq)

    wturn(0, 0)
    wturn(0, 1)
    xfwd(0, chip(3, 0))
    xfwd(0, chip(1, 0))
    xfwd(0, chip(0, 1))
    xown(1)
    wwait(chip(3, 0), 1)
    wwait(chip(1, 0), 0)
    for h in (0, 1):
        k = chip(0, 1)
        wwait(k, h)
        wput(k, chip(3, 1), zp, h)
        wput(k, chip(1, 1), zm, h)
    xfwd(0, chip(2, 0))
    wwait(chip(2, 0), 0)
    wwait(chip(2, 0), 1)
    xsib(0, range(0, 4))
    blocks(0, 0, 4, 0, 4)

    wturn(1, 0)
    xfwd(0, chip(3, 1))
    xfwd(0, chip(1, 1))
    wturn(1, 1)

    wait_in(dirg.at[chip(0, 1)], dr_sem.at[chip(0, 1)])
    for r in (0, 1):
        k = chip(0, r)
        dput(k, chip(2, r), z2)
        dput(k, chip(3, r), zp)
        dput(k, chip(1, r), zm)
    xfwd(1, chip(3, 0))
    xfwd(1, chip(1, 0))
    xfwd(1, chip(0, 1))
    xfwd(0, chip(2, 1))
    xsib(0, range(4, 8))
    blocks(0, 4, 8, 0, 4)

    xfwd(1, chip(2, 0))
    xfwd(1, chip(3, 1))
    xfwd(1, chip(1, 1))
    spread0(resid, 0, *RES)
    spread0(resid, 1, *RES)
    xsib(1, range(0, 4))
    blocks(1, 0, 4, 0, 4)
    wwait(chip(3, 1), 1)
    wwait(chip(1, 1), 0)
    wwait(chip(2, 1), 0)
    wwait(chip(2, 1), 1)
    blocks(0, 0, 8, 4, 8)
    xfwd(1, chip(2, 1))
    blocks(1, 0, 4, 4, 8)
    spread1(resid, 0, *RES)
    spread1(resid, 1, *RES)
    for r in (0, 1):
        for a in (3, 1, 2):
            wait_in(dirg.at[chip(a, r)], dr_sem.at[chip(a, r)])
    for j in range(8):
        dirt[j * 256:(j + 1) * 256, :] = dirg[j].astype(F32).T.astype(BF)
    xsib(1, range(4, 8))

    for i in range(4):
        t = tdot(0, 2 * i)
        block(1, 4 + i, 0, 8)
        tput(0, 2 * i, t)
        if i:
            tsum(0, 2 * i - 2)
            tsum(0, 2 * i - 1)
    tput(1, 0, tdot(1, 0, 4), 4)
    tsum(0, 6)
    tsum(0, 7)
    tput(1, 4, tdot(1, 4, 4), 4)
    for q in range(4):
        tsum(1, q)
    curvature(0)
    for q in range(4, 8):
        tsum(1, q)
    for p in (0, 1):
        for b in (0, 1):
            spread2(resid, p, b, *RES)
    for p in (0, 1):
        spread3(resid, p, RES[1])

    def share(v, j, own, send, recv, s_sem, r_sem):
        if j == 0:
            own[...] = v[0:147]
        else:
            a, b = RING[j]
            to = chip(-a, b)
            send[j] = v.astype(BF)
            put(send.at[j], recv.at[to], s_sem, r_sem.at[to], dev(dz=a, dyh=b))

    def cols(j):
        return slice(j * 256, (j + 1) * 256)

    order = (7, 5, 6, 4, 3, 1, 2, 0)
    for i, j in enumerate(order):
        v = jnp.dot(resid[:, 0:2048], fa[:, cols(j)], preferred_element_type=F32)
        v = v + jnp.dot(resid[:, 2048:4096], fb[:, cols(j)], preferred_element_type=F32)
        a, b = RING[j]
        if j == 0:
            grad_ref[...] = v[0:147]
        elif a == 0:
            gkeep[...] = v
        else:
            gsend[j] = v.astype(BF)
            to = chip(-a, b)
            put(gsend.at[j], grecv.at[to], gs_sem, gr_sem.at[to], dev(dz=a))
        if i == 2:
            curvature(1)
            spread1(curv, 0, *CUR)
        if i == 5:
            spread2(curv, 0, 0, *CUR)
        if i == 7:
            spread1(curv, 1, *CUR)
    spread2(curv, 0, 1, *CUR)
    spread3(curv, 0, CUR[1])
    for i, j in enumerate(order):
        hacc[:, cols(j)] = jnp.dot(curv[:, 0:2048], fa[:, cols(j)], preferred_element_type=F32)
        if i == 3:
            spread2(curv, 1, 0, *CUR)
    spread2(curv, 1, 1, *CUR)
    far = gkeep[...]
    for a in (3, 1, 2):
        k = chip(a, 1)
        wait_in(grecv.at[k], gr_sem.at[k])
        far = far + grecv[k].astype(F32)
    k = chip(0, 1)
    gsend[k] = far.astype(BF)
    put(gsend.at[k], grecv.at[k], gs_sem, gr_sem.at[k], yq)
    spread3(curv, 1, CUR[1])
    for j in order:
        v = hacc[:, cols(j)] + jnp.dot(curv[:, 2048:4096], fb[:, cols(j)], preferred_element_type=F32)
        share(v, j, hess_ref, hsend, hrecv, hs_sem, hr_sem)

    g = grad_ref[...]
    for k in (chip(3, 0), chip(1, 0), chip(2, 0), chip(0, 1)):
        wait_in(grecv.at[k], gr_sem.at[k])
        g = g + grecv[k].astype(F32)[0:147]
    grad_ref[...] = g
    h = hess_ref[...] + damp_ref[0] * dir_ref[...].astype(F32)
    for k in range(1, 8):
        wait_in(hrecv.at[k], hr_sem.at[k])
        h = h + hrecv[k].astype(F32)[0:147]
    hess_ref[...] = h

    for c in sends:
        c.wait_send()


def on_device(inputs, probs, labels, proj_weight, phase, direction, damping):
    vmem = pl.BlockSpec(memory_space=pltpu.VMEM)
    dma = pltpu.SemaphoreType.DMA
    out = jax.ShapeDtypeStruct(direction.shape, F32)
    return pl.pallas_call(
        kernel,
        out_shape=(out, out),
        in_specs=[vmem] * 6 + [pl.BlockSpec(memory_space=pltpu.SMEM)],
        out_specs=(vmem, vmem),
        scratch_shapes=[
            pltpu.VMEM((2, 16, HALF, KX), BF),
            pltpu.VMEM((8, KX, 256), BF),
            pltpu.VMEM((2048, 2048), BF),
            pltpu.VMEM((2048, 2048), BF),
            pltpu.VMEM((8, CP, 256), BF),
            pltpu.VMEM((2048, CP), BF),
            pltpu.VMEM((2, 8, CP, HALF), F32),
            pltpu.VMEM((2, 8, CP, HALF), BF),
            pltpu.VMEM((2, 8, CP, HALF), BF),
            pltpu.VMEM((2, 8, CP, HALF), BF),
            pltpu.VMEM((2, 8, CP, HALF), BF),
            pltpu.VMEM((CP, 4096), BF),
            pltpu.VMEM((CP, 4096), BF),
            pltpu.VMEM((8, CP, 256), BF),
            pltpu.VMEM((8, CP, 256), BF),
            pltpu.VMEM((8, CP, 256), BF),
            pltpu.VMEM((8, CP, 256), BF),
            pltpu.VMEM((CP, 2048), F32),
            pltpu.VMEM((CP, 256), F32),
            dma((40,)), dma((2, 16, 2)), dma((20,)), dma((8, 2)), dma((8,)), dma((8,)),
            dma((16,)), dma((2, 8)), dma((16,)), dma((2, 8)),
            dma((32,)), dma((2, 16)), dma((32,)), dma((2, 16)),
            dma((8,)), dma((8,)), dma((8,)), dma((8,)),
        ],
        compiler_params=pltpu.CompilerParams(
            collective_id=0, has_side_effects=True, vmem_limit_bytes=56 * 1024 * 1024),
    )(inputs, probs, labels.reshape(1, -1), proj_weight, phase, direction, damping)


def solution(mesh):
    placed = (
        P(None, ("samp", "feat")),
        P(None, ("samp", "feat")),
        P(("samp", "feat")),
        P(None, ("feat", "samp")),
        P(None, ("feat", "samp")),
        P(None, ("feat", "samp")),
        P(),
    )
    return jax.shard_map(
        on_device,
        mesh=mesh,
        in_specs=placed,
        out_specs=(P(None, ("feat", "samp")), P(None, ("feat", "samp"))),
        check_vma=False,
    )
```

time: 730 us -> 92.9 us (0.13)
  waiting for transfers between devices: 350 us -> 0 us
  matrix products: 297 us -> 0 us
  Pallas kernels: 0 us -> 89.2 us
  blocking collectives: 56.4 us -> 0 us
  between operations: 14.9 us -> 1.3 us
    dot_general x32 -> x0, matrix products: 297 us -> none  [the longest x8 133 us: first_late(): piece = jnp.dot(dir_all, feats, preferred_element_type=jnp.float32)]
    reduce_scatter x2 -> x0, waiting for transfers between devices: 147 us -> none  [the longest x1 75.7 us: on_device(): lax.psum_scatter(grad_acc, 'samp', scatter_dimension=1, tiled=True)]
    psum x1 -> x0, waiting for transfers between devices: 119 us -> none  [on_device(): total = lax.psum(tangent.astype(jnp.bfloat16), 'feat').astype(jnp.float32)]
    pallas_call x0 -> x1, Pallas kernels: none -> 89.2 us  [on_device(): pl.pallas_call(kernel, out_shape=(out, out), in_specs=[vmem] * 6 + [pl.Bl...]
    all_gather x4 -> x0, waiting for transfers between devices: 81.6 us -> none  [the longest x1 43.8 us: on_device(): lax.all_gather(inputs, 'feat', axis=1, tiled=True)]
    all_gather x2 -> x0, blocking collectives: 56.4 us -> none  [the longest x1 34.2 us: on_device(): lax.all_gather(direction, 'samp', axis=1, tiled=True)]
  transfers between devices with their start and end apart: 7 -> 0, of which waited for: 6 -> 0; matrix products, arithmetic and copies ran while one was open for 19% -> 0% of each run, Pallas kernels for 0% -> 0%
where the time goes in v2:
time: 92.9 us; the launch traced here: 92.8 us
  Pallas kernels  89.2 us (96%)
  local copies, waits for them, and re-layouts  2.29 us (2%)
  between operations  1.3 us (1%)
    pallas_call x1, Pallas kernels, on_device(): pl.pallas_call(kernel, out_shape=(out, out), in_specs=[vmem] * 6 + [pl.Bl...  89.2 us
    unnamed x4, local copies, waits for them, and re-layouts  2.29 us

profile of v2, /device:TPU:1, one launch (start us, length us, event | category | flops | bytes accessed | tf_op | source)
XLA Modules:
  0.0 92.8 jit_solution(12159492810359498457)
XLA Ops:
  1.3 89.2 %shard_map.86 = (f32[147,256]{1,0:T(8,128)}, f32[147,256]{1,0:T(8,128)}) custom-call(bf16[440,256]{1,0:T(8,128)(2,1)} %x_ref.1, bf16[147,256]{1,0:T(8,128)(2,1)} %prob_ref.1, s32[1,256]{1,0:T(1,128)} %bitcast.1, bf16[440,256]{1,0:T(8,128)(2,1)} %w_ref.1, bf16[1,256]{1,0:T(2,128)(2,1)} %ph_ref.1, bf16[147,256]{1,0:T(8,128)(2,1)} %dir_ref.1, f32[1]{0:T(128)S(6)} %copy.11.damp_ref), custom_call_target="tpu_custom_call" | custom-call | tf_op jit(solution)/shard_map/pallas_call | solution.py:403
  90.5 0.0 copy-start
  90.5 1.6 %copy.12 = f32[147,256]{1,0:T(8,128)} copy(f32[147,256]{1,0:T(8,128)} %get-tuple-element.4) | data formatting | bytes 301056
  92.1 0.0 copy-done
  92.1 0.7 copy.13
Async XLA Ops:
  90.5 1.6 %copy-start = (f32[147,256]{1,0:T(8,128)S(1)}, f32[147,256]{1,0:T(8,128)}, u32[]{:S(2)}) copy-start(f32[147,256]{1,0:T(8,128)} %get-tuple-element.5) | copy-start | bytes 451588
